TPU v7x, 32 devices: a whole 2x2x4 slice. The times are simulated.
32 devices in a mesh: groups: 2 (over y), rows: 4 (over z), zero: 4 (over x, core).
Axes of the slice: x: 2, y: 2, z: 4, core: 2. Of those that a mesh axis runs over, the one named last changes fastest.
Arguments:
- latents: bfloat16 [8, 320, 32, 128], P(('groups', 'zero'), None, 'rows'), parts along dimension 0, may hold values from -40 to 40
- time_shift: float32 [8, 320], P(('groups', 'zero')), parts along dimension 0, may hold values from -4 to 4
- conv_first: bfloat16 [320, 9, 320], P('zero'), may hold values from -0.109375 to 0.109375
- conv_second: bfloat16 [320, 9, 320], P('zero'), may hold values from -0.1875 to 0.1875
- norm_gains: float32 [2, 320], replicated, may hold values from 0.5 to 1.5
- norm_biases: float32 [2, 320], replicated, may hold values from -3 to 3
- grad_output: bfloat16 [8, 320, 32, 128], P(('groups', 'zero'), None, 'rows'), parts along dimension 0, may hold values from -40 to 40
Outputs:
- block_out: bfloat16 [8, 320, 32, 128], P(('groups', 'zero'), None, 'rows'), parts along dimension 0
- grad_input: bfloat16 [8, 320, 32, 128], P(('groups', 'zero'), None, 'rows'), parts along dimension 0
- grad_time: float32 [8, 320], P(('groups', 'zero')), parts along dimension 0
- grad_conv_first: float32 [640, 9, 320], P(('groups', 'zero')), parts along dimension 0
- grad_conv_second: float32 [640, 9, 320], P(('groups', 'zero')), parts along dimension 0
- grad_norms: float32 [8, 320], P('groups'), parts along dimension 0
There are 2 independent parts, one for each index of `groups`. A program takes and returns all parts, laid end to end along the dimension named above; an argument that names none is the same for every part. Nothing has to cross between parts.
All inputs are finite; a program needn't handle non-finite values.
Results may differ from a plain program's by a relative error of at most 0.0056.
Values may be sent and summed in bfloat16 or wider, within the bound.
A program may use at most 128 MiB of HBM per device.

v0:
```python
import jax
import jax.numpy as jnp
from jax import lax
from jax.sharding import PartitionSpec as P

NORM_GROUPS = 32
EPSILON = 1e-05


def with_halo(value, sides, width):
    for axis, dim in sides:
        devices, length = (lax.axis_size(axis), value.shape[dim])
        up = [(i, (i + 1) % devices) for i in range(devices - 1)]
        down = [(j, i) for i, j in up]
        last = lax.slice_in_dim(value, length - width, length, axis=dim)
        first = lax.slice_in_dim(value, 0, width, axis=dim)
        before = lax.ppermute(last, axis, up)
        after = lax.ppermute(first, axis, down)
        value = jnp.concatenate([before, value, after], axis=dim)
    return value


def shifted_stack(padded, flipped):
    height = padded.shape[2] - 2
    width = padded.shape[3]
    widened = jnp.pad(padded, ((0, 0), (0, 0), (0, 0), (1, 1)))
    slices = [
        widened[:, :, tap_row : tap_row + height, tap_col : tap_col + width]
        for tap_row in range(3)
        for tap_col in range(3)
    ]
    if flipped:
        slices = slices[::-1]
    return jnp.stack(slices, axis=1)


def with_faces(field):
    return with_halo(field, (("rows", 2),), 1)


def group_stats(values):
    images, channels, height, width = values.shape
    grouped = values.reshape(images, NORM_GROUPS, channels // NORM_GROUPS, height, width)
    members = channels // NORM_GROUPS * height * width * lax.axis_size("rows")
    totals, squares = lax.psum(
        (jnp.sum(grouped, axis=(2, 3, 4)), jnp.sum(grouped * grouped, axis=(2, 3, 4))), "rows"
    )
    average = totals / members
    centered = grouped - average[:, :, None, None, None]
    variance = squares / members - average * average
    scaling = lax.rsqrt(variance + EPSILON)
    return ((centered * scaling[:, :, None, None, None]).reshape(values.shape), scaling)


def norm_backward(grad_normed, normed, scaling):
    images, channels, height, width = normed.shape
    shape = (images, NORM_GROUPS, channels // NORM_GROUPS, height, width)
    members = channels // NORM_GROUPS * height * width * lax.axis_size("rows")
    grouped_grad = grad_normed.reshape(shape)
    grouped_norm = normed.reshape(shape)
    group_sum, cross_sum = lax.psum(
        (
            jnp.sum(grouped_grad, axis=(2, 3, 4)),
            jnp.sum(grouped_grad * grouped_norm, axis=(2, 3, 4)),
        ),
        "rows",
    )
    result = scaling[:, :, None, None, None] * (
        grouped_grad
        - (group_sum / members)[:, :, None, None, None]
        - grouped_norm * (cross_sum / members)[:, :, None, None, None]
    )
    return result.reshape(normed.shape)


def silu_slope(pre_values):
    logistic = jax.nn.sigmoid(pre_values)
    return logistic * (1.0 + pre_values * (1.0 - logistic))


def forward_conv(stacked, shard):
    return jnp.einsum(
        "otc,ntchw->nohw",
        lax.all_gather(shard, "zero", axis=0, tiled=True),
        stacked,
        preferred_element_type=jnp.float32,
    )


def backward_conv(stacked_grad, shard):
    return jnp.einsum(
        "otc,ntohw->nchw",
        lax.all_gather(shard, "zero", axis=0, tiled=True),
        stacked_grad,
        preferred_element_type=jnp.float32,
    )


def weight_gradient(cotangent, stacked):
    share = lax.psum_scatter(
        jnp.einsum("nohw,ntchw->otc", cotangent, stacked, preferred_element_type=jnp.float32),
        "zero",
        scatter_dimension=0,
        tiled=True,
    )
    return lax.psum(share, "rows")


def local(latents, time_shift, conv_first, conv_second, norm_gains, norm_biases, grad_output):
    gain_first = norm_gains[0][None, :, None, None]
    gain_second = norm_gains[1][None, :, None, None]
    bias_first = norm_biases[0][None, :, None, None]
    bias_second = norm_biases[1][None, :, None, None]
    normed_first, scale_first = group_stats(latents.astype(jnp.float32))
    pre_first = gain_first * normed_first + bias_first
    act_first = jax.nn.silu(pre_first).astype(jnp.bfloat16)
    stack_first = shifted_stack(with_faces(act_first), False)
    conv_out = forward_conv(stack_first, conv_first)
    hidden = (conv_out + time_shift[:, :, None, None]).astype(jnp.bfloat16)
    normed_second, scale_second = group_stats(hidden.astype(jnp.float32))
    pre_second = gain_second * normed_second + bias_second
    act_second = jax.nn.silu(pre_second).astype(jnp.bfloat16)
    stack_second = shifted_stack(with_faces(act_second), False)
    second_out = forward_conv(stack_second, conv_second)
    block_out = (latents.astype(jnp.float32) + second_out).astype(jnp.bfloat16)
    grad_conv_second = weight_gradient(grad_output, stack_second)
    stack_grad = shifted_stack(with_faces(grad_output), True)
    back_second = backward_conv(stack_grad, conv_second)
    slope_second = back_second * silu_slope(pre_second)
    grad_hidden = norm_backward(gain_second * slope_second, normed_second, scale_second)
    grad_time = lax.psum(jnp.sum(grad_hidden, axis=(2, 3)), "rows")
    hidden_grad = grad_hidden.astype(jnp.bfloat16)
    grad_conv_first = weight_gradient(hidden_grad, stack_first)
    stack_hidden = shifted_stack(with_faces(hidden_grad), True)
    back_first = backward_conv(stack_hidden, conv_first)
    slope_first = back_first * silu_slope(pre_first)
    grad_latent = norm_backward(gain_first * slope_first, normed_first, scale_first)
    grad_input = (grad_output.astype(jnp.float32) + grad_latent).astype(jnp.bfloat16)
    local_terms = jnp.stack(
        [
            jnp.sum(slope_first * normed_first, axis=(0, 2, 3)),
            jnp.sum(slope_first, axis=(0, 2, 3)),
            jnp.sum(slope_second * normed_second, axis=(0, 2, 3)),
            jnp.sum(slope_second, axis=(0, 2, 3)),
        ]
    )
    grad_norms = lax.psum(local_terms, ("rows", "zero"))
    return (block_out, grad_input, grad_time, grad_conv_first, grad_conv_second, grad_norms)


def solution(mesh):
    placed = (
        P(("groups", "zero"), None, "rows", None),
        P(("groups", "zero"), None),
        P("zero", None, None),
        P("zero", None, None),
        P(),
        P(),
        P(("groups", "zero"), None, "rows", None),
    )
    return jax.shard_map(
        local,
        mesh=mesh,
        in_specs=placed,
        out_specs=(
            P(("groups", "zero"), None, "rows", None),
            P(("groups", "zero"), None, "rows", None),
            P(("groups", "zero"), None),
            P(("groups", "zero"), None, None),
            P(("groups", "zero"), None, None),
            P("groups", None),
        ),
        check_vma=False,
    )
```

profile of v0, /device:TPU:0, one launch (start us, length us, event | category | flops | bytes accessed | tf_op | source)
XLA Modules:
  0.0 314.7 jit_solution(3994753162945767644)
XLA Ops:
  8.0 1.4 convert_reduce_fusion
  9.8 13.5 %all-reduce.7 = (f32[1,32]{1,0:T(1,128)S(1)}, f32[1,32]{1,0:T(1,128)S(1)}) all-reduce(f32[1,32]{1,0:T(1,128)S(1)} %bitcast.372, f32[1,32]{1,0:T(1,128)S(1)} %bitcast.371), channel_id=1, replica_groups=mesh['groups'=2,'rows'=4,'zero'=4] {'rows'}, use_global_device_ids=true, to_apply=%region_5.6 | all-reduce | flops 64 | bytes 512 | tf_op jit(solution)/shard_map/psum | solution.py:45
  25.1 1.3 collective-permute-start
  26.4 1.3 collective-permute-start.1
  27.9 4.6 %collective-permute-start.4 = (bf16[1,320,1,128]{3,1,2,0:T(8,128)(2,1)S(1)}, bf16[1,320,1,128]{3,1,2,0:T(8,128)(2,1)S(1)}, u32[]{:S(2)}, u32[]{:S(2)}) collective-permute-start(bf16[1,320,1,128]{3,1,2,0:T(8,128)(2,1)S(1)} %get-tuple-element.56), channel_id=1, source_target_pairs={{0,4},{4,8},{8,12},{1,5},{5,9},{9,13},{2,6},{6,10},{10,14},{3,7},{... | collective-permute-start | bytes 245768 | tf_op jit(solution)/shard_map/ppermute | solution.py:17
  32.4 1.3 collective-permute-start.5
  36.7 2.0 collective-permute-done.5
  39.6 1.1 fusion.130
  40.7 1.0 fusion.129
  41.7 1.0 fusion.127
  42.7 1.1 fusion.126
  43.9 1.0 bitcast_dynamic-update-slice_fusion.2
  44.8 1.0 fusion.125
  45.8 1.1 fusion.124
  46.9 1.0 fusion.123
  48.3 2.6 copy-done.4
  50.8 1.0 fusion.121
  51.8 5.8 %convert_reduce_fusion.1 = (f32[320]{0:T(512)S(1)}, f32[320]{0:T(512)S(1)}, bf16[1,8,128,320]{2,3,1,0:T(8,128)(2,1)S(1)}) fusion(f32[320]{0:T(512)S(1)} %reduce.34, bf16[1,9,320,8,128]{4,2,1,3,0:T(8,128)(2,1)} %copy-done.4, bf16[320,9,320]{2,0,1:T(8,128)(2,1)} %all-gather.3.cloned.1.call-done), kind=kOutput, calls=%fused_computation.26 | convolution fusion | flops 1889402368 | bytes 8400640 | tf_op jit(solution)/shard_map/otc,ntchw->nohw/dot_general | solution.py:82
  58.0 9.6 %all-reduce.6 = (f32[1,32]{1,0:T(1,128)S(1)}, f32[1,32]{1,0:T(1,128)S(1)}) all-reduce(f32[1,32]{1,0:T(1,128)S(1)} %bitcast.373, f32[1,32]{1,0:T(1,128)S(1)} %bitcast.369), channel_id=1, replica_groups=mesh['groups'=2,'rows'=4,'zero'=4] {'rows'}, use_global_device_ids=true, to_apply=%region_11.12 | all-reduce | flops 64 | bytes 512 | tf_op jit(solution)/shard_map/psum | solution.py:45
  68.0 6.4 %fusion.83 = (f32[320]{0:T(512)S(1)}, f32[320]{0:T(512)S(1)}, f32[320]{0:T(512)S(1)}, f32[320]{0:T(512)S(1)}, f32[1,320,8,128]{3,1,2,0:T(8,128)S(1)}) fusion(bf16[1,8,128,320]{2,3,1,0:T(8,128)(2,1)S(1)} %get-tuple-element.66, f32[320]{0:T(512)S(1)} %mul.235, f32[320]{0:T(512)S(1)} %sub.127, f32[320]{0:T(512)S(1)} %get-tuple-element.70, ...), kind=kOutput, calls=%fused_computation.64 | convolution fusion | flops 1893989376 | bytes 9717760 | tf_op jit(solution)/shard_map/otc,ntohw->nchw/dot_general | solution.py:91
  74.8 9.4 %all-reduce.5 = (f32[1,32]{1,0:T(1,128)S(1)}, f32[1,32]{1,0:T(1,128)S(1)}) all-reduce(f32[1,32]{1,0:T(1,128)S(1)} %bitcast.374, f32[1,32]{1,0:T(1,128)S(1)} %bitcast.370), channel_id=1, replica_groups=mesh['groups'=2,'rows'=4,'zero'=4] {'rows'}, use_global_device_ids=true, to_apply=%region_17.18 | all-reduce | flops 64 | bytes 512 | tf_op jit(solution)/shard_map/psum | solution.py:61
  84.6 2.1 fusion.154
  86.7 2.9 collective-permute-start.2
  89.6 1.3 collective-permute-start.3
  91.6 4.3 %collective-permute-done.3 = bf16[1,320,1,128]{3,1,2,0:T(8,128)(2,1)S(1)} collective-permute-done((bf16[1,320,1,128]{3,1,2,0:T(8,128)(2,1)S(1)}, bf16[1,320,1,128]{3,1,2,0:T(8,128)(2,1)S(1)}, u32[]{:S(2)}, u32[]{:S(2)}) %collective-permute-start.3) | collective-permute-done | bytes 81952 | tf_op jit(solution)/shard_map/ppermute | solution.py:18
  98.6 4.8 %fusion.4 = f32[9,320,320,1]{2,1,3,0:T(8,128)} fusion(bf16[1,9,320,8,128]{4,2,3,1,0:T(8,128)(2,1)S(1)} %fusion.131, bf16[320,8,128]{2,1,0:T(8,128)(2,1)S(1)} %bitcast.365), kind=kOutput, calls=%fused_computation.4 | convolution fusion | flops 1887436800 | bytes 10240000 | tf_op jit(solution)/shard_map/nohw,ntchw->otc/dot_general | solution.py:101
  103.5 5.6 %copy.103 = f32[320,2880]{1,0:T(8,128)} copy(f32[320,2880]{0,1:T(8,128)} %bitcast.366) | data formatting | bytes 7372800
  109.1 8.1 %fusion.17 = f32[320,9,320]{2,0,1:T(8,128)} fusion(bf16[1,9,320,8,128]{4,2,1,3,0:T(8,128)(2,1)} %copy-done.4, bf16[1,320,8,128]{3,1,2,0:T(8,128)(2,1)S(1)} %get-tuple-element.52), kind=kOutput, calls=%fused_computation.23 | convolution fusion | flops 1887436800 | bytes 10240000 | tf_op jit(solution)/shard_map/nohw,ntchw->otc/dot_general | solution.py:101
  117.3 1.9 collective-permute-start.6
  119.3 1.5 collective-permute-start.7
  121.3 4.3 %collective-permute-done.7 = bf16[1,320,1,128]{3,1,2,0:T(8,128)(2,1)S(1)} collective-permute-done((bf16[1,320,1,128]{3,1,2,0:T(8,128)(2,1)S(1)}, bf16[1,320,1,128]{3,1,2,0:T(8,128)(2,1)S(1)}, u32[]{:S(2)}, u32[]{:S(2)}) %collective-permute-start.7) | collective-permute-done | bytes 81952 | tf_op jit(solution)/shard_map/ppermute | solution.py:18
  126.5 1.1 fusion.120
  128.5 1.0 fusion.117
  129.4 1.1 fusion.116
  131.5 1.0 fusion.115
  132.4 1.1 fusion.114
  135.4 14.0 %reduce-scatter.7.cloned.1.call-done = f32[80,2880]{1,0:T(8,128)} async-done(((f32[320,2880]{1,0:T(8,128)}), f32[80,2880]{1,0:T(8,128)}) %reduce-scatter.7.cloned.1.call-update) | async-done | bytes 921616
  149.4 2.8 copy.104
  152.1 45.8 %reduce-scatter.5.cloned.1.call-done = f32[80,9,320]{2,0,1:T(8,128)} async-done(((f32[320,9,320]{2,0,1:T(8,128)}), f32[80,9,320]{2,0,1:T(8,128)}) %reduce-scatter.5.cloned.1.call-update) | async-done | bytes 921616 | tf_op jit(solution)/shard_map/reduce_scatter | solution.py:100
  198.0 6.4 %fusion.105 = (f32[320]{0:T(512)S(1)}, f32[320]{0:T(512)S(1)}, f32[320]{0:T(512)S(1)}, f32[320]{0:T(512)S(1)}, f32[1,320,8,128]{3,1,2,0:T(8,128)S(1)}) fusion(f32[320]{0:T(512)S(1)} %mul.226, f32[320]{0:T(512)S(1)} %sub.121, bf16[1,320,8,128]{3,2,1,0:T(8,128)(2,1)S(1)} %copy-done, f32[320]{0:T(512)S(1)} %get-tuple-element.69, ...), kind=kOutput, calls=%fused_computation.86 | convolution fusion | flops 1893989376 | bytes 9717760 | tf_op jit(solution)/shard_map/otc,ntohw->nchw/dot_general | solution.py:91
  204.8 12.6 %all-reduce.4 = (f32[1,32]{1,0:T(1,128)S(1)}, f32[1,32]{1,0:T(1,128)S(1)}, f32[1,320]{1,0:T(1,128)}) all-reduce(f32[1,32]{1,0:T(1,128)S(1)} %bitcast.368, f32[1,32]{1,0:T(1,128)S(1)} %bitcast.367, f32[1,320]{1,0:T(1,128)S(1)} %reduce_sum.224), channel_id=1, replica_groups=mesh['groups'=2,'rows'=4,'zero'=4] {'rows'}, use_global_device_ids=true, to_apply=%region_23.24 | all-reduce | flops 384 | bytes 3072 | tf_op jit(solution)/shard_map/psum | solution.py:61
  218.4 1.3 copy.93
  219.7 5.0 %fusion.59 = bf16[1,320,8,128]{3,1,2,0:T(8,128)(2,1)S(1)} fusion(bf16[1,9,320,8,128]{4,2,3,1,0:T(8,128)(2,1)} %copy-done.5, bf16[320,9,320]{2,0,1:T(8,128)(2,1)S(1)} %copy-done.7, bf16[1,320,8,128]{3,2,1,0:T(8,128)(2,1)S(1)} %copy-done), kind=kOutput, calls=%fused_computation.44 | convolution fusion | flops 1888419840 | bytes 9052160 | tf_op jit(solution)/shard_map/otc,ntchw->nohw/dot_general | solution.py:82
  224.7 1.3 copy.92
  225.9 33.0 %psum.95 = f32[4,320]{1,0:T(4,128)} all-reduce(f32[4,320]{1,0:T(4,128)S(1)} %pad_maximum_fusion.8), channel_id=1, replica_groups=mesh['groups'=2,'rows'=4,'zero'=4] {'rows','zero'}, use_global_device_ids=true, to_apply=%region_34.35 | all-reduce | flops 1280 | bytes 10240 | tf_op jit(solution)/shard_map/psum | solution.py:147
  259.0 45.2 %all-reduce.11.cloned.1.call-done = (f32[80,9,320]{2,0,1:T(8,128)}, f32[80,9,320]{0,2,1:T(8,128)}) async-done(((f32[80,9,320]{2,0,1:T(8,128)}, f32[80,9,320]{0,2,1:T(8,128)}), (f32[80,9,320]{2,0,1:T(8,128)}, f32[80,9,320]{0,2,1:T(8,128)})) %all-reduce.11.cloned.1.call-update) | async-done | bytes 1843216 | tf_op jit(solution)/shard_map/psum | solution.py:106
  304.2 3.0 copy.94
  307.2 1.0 copy.155
  (111 shorter events, 19.0 us)
Async XLA Ops:
  7.2 17.3 %copy-start = (bf16[1,320,8,128]{3,2,1,0:T(8,128)(2,1)S(1)}, bf16[1,320,8,128]{3,2,1,0:T(8,128)(2,1)}, u32[]{:S(2)}) copy-start(bf16[1,320,8,128]{3,2,1,0:T(8,128)(2,1)} %param.7) | copy-start | bytes 1966084
  7.2 20.6 %copy-start.1 = (bf16[1,320,8,128]{3,2,1,0:T(8,128)(2,1)S(1)}, bf16[1,320,8,128]{3,2,1,0:T(8,128)(2,1)}, u32[]{:S(2)}) copy-start(bf16[1,320,8,128]{3,2,1,0:T(8,128)(2,1)} %param.13) | copy-start | bytes 1966084
  7.2 44.6 %all-gather.3.cloned.1.call-start = ((), (), s32[]{:S(2)}) async-start(), calls=%async_computation.2 | async-start | bytes 2764800 | tf_op jit(solution)/shard_map/all_gather | solution.py:84
  7.9 60.1 %all-gather.5.cloned.1.call-start = ((), (), s32[]{:S(2)}) async-start(), calls=%async_computation.3 | async-start | bytes 2764800 | tf_op jit(solution)/shard_map/all_gather | solution.py:84
  24.4 9.3 %copy-start.6 = (f32[1,320]{1,0:T(1,128)S(1)}, f32[1,320]{1,0:T(1,128)}, u32[]{:S(2)}) copy-start(f32[1,320]{1,0:T(1,128)} %param.8) | copy-start | bytes 3844
  25.1 8.7 %collective-permute-start = (bf16[1,320,1,128]{3,1,2,0:T(8,128)(2,1)S(1)}, bf16[1,320,1,128]{3,1,2,0:T(8,128)(2,1)S(1)}, u32[]{:S(2)}, u32[]{:S(2)}) collective-permute-start(bf16[1,320,1,128]{3,1,2,0:T(8,128)(2,1)S(1)} %get-tuple-element.60), channel_id=1, source_target_pairs={{0,4},{4,8},{8,12},{1,5},{5,9},{9,13},{2,6},{6,10},{10,14},{3,7},{... | collective-permute-start | bytes 245768 | tf_op jit(solution)/shard_map/ppermute | solution.py:17
  26.4 7.4 %collective-permute-start.1 = (bf16[1,320,1,128]{3,1,2,0:T(8,128)(2,1)S(1)}, bf16[1,320,1,128]{3,1,2,0:T(8,128)(2,1)S(1)}, u32[]{:S(2)}, u32[]{:S(2)}) collective-permute-start(bf16[1,320,1,128]{3,1,2,0:T(8,128)(2,1)S(1)} %get-tuple-element.61), channel_id=1, source_target_pairs={{4,0},{8,4},{12,8},{5,1},{9,5},{13,9},{6,2},{10,6},{14,10},{7,3},{... | collective-permute-start | bytes 245768 | tf_op jit(solution)/shard_map/ppermute | solution.py:18
  27.9 8.9 %collective-permute-start.4 = (bf16[1,320,1,128]{3,1,2,0:T(8,128)(2,1)S(1)}, bf16[1,320,1,128]{3,1,2,0:T(8,128)(2,1)S(1)}, u32[]{:S(2)}, u32[]{:S(2)}) collective-permute-start(bf16[1,320,1,128]{3,1,2,0:T(8,128)(2,1)S(1)} %get-tuple-element.56), channel_id=1, source_target_pairs={{0,4},{4,8},{8,12},{1,5},{5,9},{9,13},{2,6},{6,10},{10,14},{3,7},{... | collective-permute-start | bytes 245768 | tf_op jit(solution)/shard_map/ppermute | solution.py:17
  32.4 6.3 %collective-permute-start.5 = (bf16[1,320,1,128]{3,1,2,0:T(8,128)(2,1)S(1)}, bf16[1,320,1,128]{3,1,2,0:T(8,128)(2,1)S(1)}, u32[]{:S(2)}, u32[]{:S(2)}) collective-permute-start(bf16[1,320,1,128]{3,1,2,0:T(8,128)(2,1)S(1)} %get-tuple-element.57), channel_id=1, source_target_pairs={{4,0},{8,4},{12,8},{5,1},{9,5},{13,9},{6,2},{10,6},{14,10},{7,3},{... | collective-permute-start | bytes 245768 | tf_op jit(solution)/shard_map/ppermute | solution.py:18
  33.7 115.6 %reduce-scatter.7.cloned.1.call-start = ((), (), s32[]{:S(2)}) async-start(), calls=%async_computation.5 | async-start | bytes 4710400
  48.2 2.6 copy-start.4
  57.6 16.8 %copy-start.3 = (bf16[1,8,128,320]{2,3,1,0:T(8,128)(2,1)}, bf16[1,8,128,320]{2,3,1,0:T(8,128)(2,1)S(1)}, u32[]{:S(2)}) copy-start(bf16[1,8,128,320]{2,3,1,0:T(8,128)(2,1)S(1)} %get-tuple-element.66) | copy-start | bytes 1966084
  86.7 5.0 %collective-permute-start.2 = (bf16[1,320,1,128]{3,1,2,0:T(8,128)(2,1)S(1)}, bf16[1,320,1,128]{3,1,2,0:T(8,128)(2,1)S(1)}, u32[]{:S(2)}, u32[]{:S(2)}) collective-permute-start(bf16[1,320,1,128]{3,1,2,0:T(8,128)(2,1)S(1)} %get-tuple-element.58), channel_id=1, source_target_pairs={{0,4},{4,8},{8,12},{1,5},{5,9},{9,13},{2,6},{6,10},{10,14},{3,7},{... | collective-permute-start | bytes 245768 | tf_op jit(solution)/shard_map/ppermute | solution.py:17
  89.6 6.3 %collective-permute-start.3 = (bf16[1,320,1,128]{3,1,2,0:T(8,128)(2,1)S(1)}, bf16[1,320,1,128]{3,1,2,0:T(8,128)(2,1)S(1)}, u32[]{:S(2)}, u32[]{:S(2)}) collective-permute-start(bf16[1,320,1,128]{3,1,2,0:T(8,128)(2,1)S(1)} %get-tuple-element.59), channel_id=1, source_target_pairs={{4,0},{8,4},{12,8},{5,1},{9,5},{13,9},{6,2},{10,6},{14,10},{7,3},{... | collective-permute-start | bytes 245768 | tf_op jit(solution)/shard_map/ppermute | solution.py:18
  98.6 4.9 %copy-start.5 = (bf16[1,9,320,8,128]{4,2,3,1,0:T(8,128)(2,1)}, bf16[1,9,320,8,128]{4,2,3,1,0:T(8,128)(2,1)S(1)}, u32[]{:S(2)}) copy-start(bf16[1,9,320,8,128]{4,2,3,1,0:T(8,128)(2,1)S(1)} %fusion.131) | copy-start | bytes 17694724
  109.1 88.9 %reduce-scatter.5.cloned.1.call-start = ((), (), s32[]{:S(2)}) async-start(), calls=%async_computation.4 | async-start | bytes 5529600 | tf_op jit(solution)/shard_map/reduce_scatter | solution.py:100
  117.3 186.9 %all-reduce.11.cloned.1.call-start = ((), (), s32[]{:S(2)}) async-start(), calls=%async_computation.6 | async-start | bytes 5160960 | tf_op jit(solution)/shard_map/psum | solution.py:106
  117.3 4.0 %collective-permute-start.6 = (bf16[1,320,1,128]{3,1,2,0:T(8,128)(2,1)S(1)}, bf16[1,320,1,128]{3,1,2,0:T(8,128)(2,1)S(1)}, u32[]{:S(2)}, u32[]{:S(2)}) collective-permute-start(bf16[1,320,1,128]{3,1,2,0:T(8,128)(2,1)S(1)} %get-tuple-element.54), channel_id=1, source_target_pairs={{0,4},{4,8},{8,12},{1,5},{5,9},{9,13},{2,6},{6,10},{10,14},{3,7},{... | collective-permute-start | bytes 245768 | tf_op jit(solution)/shard_map/ppermute | solution.py:17
  119.3 6.3 %collective-permute-start.7 = (bf16[1,320,1,128]{3,1,2,0:T(8,128)(2,1)S(1)}, bf16[1,320,1,128]{3,1,2,0:T(8,128)(2,1)S(1)}, u32[]{:S(2)}, u32[]{:S(2)}) collective-permute-start(bf16[1,320,1,128]{3,1,2,0:T(8,128)(2,1)S(1)} %get-tuple-element.55), channel_id=1, source_target_pairs={{4,0},{8,4},{12,8},{5,1},{9,5},{13,9},{6,2},{10,6},{14,10},{7,3},{... | collective-permute-start | bytes 245768 | tf_op jit(solution)/shard_map/ppermute | solution.py:18
  217.8 1.9 copy-start.7
  304.2 3.0 copy-start.2
Sparse Core Ops, SparseCore 0:
  9.6 25.9 all-gather.2
  37.1 23.2 all-gather.4
  109.2 40.1 reduce-scatter.6
  152.0 45.9 reduce-scatter.4
  200.3 103.8 all-reduce.10
where the time goes:
time: 315 us
  waiting for transfers between devices  118 us (37%)
  blocking collectives  78 us (25%)
  local copies, waits for them, and re-layouts  38.1 us (12%)
  matrix products  36.4 us (12%)
  starting transfers between devices  16.3 us (5%)
  between operations  14.3 us (5%)
  other arithmetic  14 us (4%)
    reduce_scatter x1, waiting for transfers between devices, weight_gradient(): lax.psum_scatter(jnp.einsum('nohw,ntchw->otc', cotangent, stacked, prefer...  45.8 us
    psum x1, waiting for transfers between devices, weight_gradient(): return lax.psum(share, 'rows')  45.2 us
    psum x1, blocking collectives, local(): grad_norms = lax.psum(local_terms, ('rows', 'zero'))  33 us
    unnamed x46, local copies, waits for them, and re-layouts  32.3 us
    psum x2, blocking collectives, group_stats(): lax.psum((jnp.sum(grouped, axis=(2, 3, 4)), jnp.sum(grouped * grouped, ax...  23 us
    psum x2, blocking collectives, norm_backward(): lax.psum((jnp.sum(grouped_grad, axis=(2, 3, 4)), jnp.sum(grouped_grad * g...  22 us
    unnamed x6, waiting for transfers between devices  14.7 us
    dot_general x2, matrix products, weight_gradient(): jnp.einsum('nohw,ntchw->otc', cotangent, stacked, preferred_element_type=...  12.9 us
  transfers between devices with their start and end apart: 13, of which 8 were waited for; matrix products, arithmetic and copies ran while one was open for 19% of the time, Pallas kernels for 0%

commit v1 on v0

--- a/solution.py
+++ b/solution.py
@@ -2,9 +2,11 @@
 import jax.numpy as jnp
 from jax import lax
 from jax.sharding import PartitionSpec as P
+from jax.lax import all_gather
 
 NORM_GROUPS = 32
 EPSILON = 1e-05
+load_spans = lambda piece_in: jnp.sum(all_gather(piece_in, "rows"), 0)
 
 
 def with_halo(value, sides, width):
@@ -103,7 +105,7 @@
         scatter_dimension=0,
         tiled=True,
     )
-    return lax.psum(share, "rows")
+    return load_spans(share)
 
 
 def local(latents, time_shift, conv_first, conv_second, norm_gains, norm_biases, grad_output):

time: 315 us -> 368 us (1.17)
  waiting for transfers between devices: 118 us -> 175 us
  local copies, waits for them, and re-layouts: 38.1 us -> 30.6 us
  other arithmetic: 14 us -> 20 us
    all_gather x0 -> x2, waiting for transfers between devices: none -> 95.6 us  [load_spans = lambda piece_in: jnp.sum(all_gather(piece_in, 'rows'), 0)]
    psum x1 -> x0, waiting for transfers between devices: 45.2 us -> none  [weight_gradient(): return lax.psum(share, 'rows')]
    unnamed x6 -> x7, waiting for transfers between devices: 14.7 us -> 45.2 us
    reduce_scatter x1, waiting for transfers between devices: 45.8 us -> 21.8 us  [weight_gradient(): lax.psum_scatter(jnp.einsum('nohw,ntchw->otc', cotangent, stacked, prefer...]
    unnamed x46 -> x44, local copies, waits for them, and re-layouts: 32.3 us -> 24.2 us
    reduce_sum x0 -> x2, other arithmetic: none -> 7.25 us  [load_spans = lambda piece_in: jnp.sum(all_gather(piece_in, 'rows'), 0)]
  transfers between devices with their start and end apart: 13 -> 14, of which waited for: 8 -> 9; matrix products, arithmetic and copies ran while one was open for 19% -> 16% of each run, Pallas kernels for 0% -> 0%
where the time goes in v1:
time: 368 us
  waiting for transfers between devices  175 us (48%)
  blocking collectives  75.2 us (20%)
  matrix products  33.9 us (9%)
  local copies, waits for them, and re-layouts  30.6 us (8%)
  other arithmetic  20 us (5%)
  starting transfers between devices  17.8 us (5%)
  between operations  14.7 us (4%)
    all_gather x2, waiting for transfers between devices, load_spans = lambda piece_in: jnp.sum(all_gather(piece_in, 'rows'), 0)  95.6 us
    unnamed x7, waiting for transfers between devices  45.2 us
    psum x1, blocking collectives, local(): grad_norms = lax.psum(local_terms, ('rows', 'zero'))  32.3 us
    unnamed x44, local copies, waits for them, and re-layouts  24.2 us
    psum x2, blocking collectives, group_stats(): lax.psum((jnp.sum(grouped, axis=(2, 3, 4)), jnp.sum(grouped * grouped, ax...  23 us
    reduce_scatter x1, waiting for transfers between devices, weight_gradient(): lax.psum_scatter(jnp.einsum('nohw,ntchw->otc', cotangent, stacked, prefer...  21.8 us
    psum x2, blocking collectives, norm_backward(): lax.psum((jnp.sum(grouped_grad, axis=(2, 3, 4)), jnp.sum(grouped_grad * g...  19.9 us
    dot_general x2, matrix products, weight_gradient(): jnp.einsum('nohw,ntchw->otc', cotangent, stacked, preferred_element_type=...  13 us
  transfers between devices with their start and end apart: 14, of which 9 were waited for; matrix products, arithmetic and copies ran while one was open for 16% of the time, Pallas kernels for 0%

profile of v1, /device:TPU:0, one launch (start us, length us, event | category | flops | bytes accessed | tf_op | source)
XLA Modules:
  0.0 367.6 jit_solution(17380237841301513601)
XLA Ops:
  8.0 1.4 convert_reduce_fusion
  9.8 13.5 %all-reduce.7 = (f32[1,32]{1,0:T(1,128)S(1)}, f32[1,32]{1,0:T(1,128)S(1)}) all-reduce(f32[1,32]{1,0:T(1,128)S(1)} %bitcast.376, f32[1,32]{1,0:T(1,128)S(1)} %bitcast.375), channel_id=1, replica_groups=mesh['groups'=2,'rows'=4,'zero'=4] {'rows'}, use_global_device_ids=true, to_apply=%region_5.6 | all-reduce | flops 64 | bytes 512 | tf_op jit(solution)/shard_map/psum | solution.py:47
  25.1 1.3 collective-permute-start
  26.4 1.3 collective-permute-start.1
  27.8 4.6 %collective-permute-start.4 = (bf16[1,320,1,128]{3,1,2,0:T(8,128)(2,1)S(1)}, bf16[1,320,1,128]{3,1,2,0:T(8,128)(2,1)S(1)}, u32[]{:S(2)}, u32[]{:S(2)}) collective-permute-start(bf16[1,320,1,128]{3,1,2,0:T(8,128)(2,1)S(1)} %get-tuple-element.54), channel_id=1, source_target_pairs={{0,4},{4,8},{8,12},{1,5},{5,9},{9,13},{2,6},{6,10},{10,14},{3,7},{... | collective-permute-start | bytes 245768 | tf_op jit(solution)/shard_map/ppermute | solution.py:19
  32.4 1.3 collective-permute-start.5
  33.8 0.9 fusion.24
  36.7 2.0 collective-permute-done.5
  39.6 1.1 fusion.130
  40.7 1.0 fusion.129
  41.7 1.0 fusion.127
  42.7 1.1 fusion.126
  43.9 1.0 bitcast_dynamic-update-slice_fusion.2
  44.9 1.0 fusion.125
  45.9 1.1 fusion.124
  47.0 1.0 fusion.123
  48.3 2.5 copy-done.3
  50.8 1.0 fusion.121
  51.8 5.8 %convert_reduce_fusion.1 = (f32[320]{0:T(512)S(1)}, f32[320]{0:T(512)S(1)}, bf16[1,8,128,320]{2,3,1,0:T(8,128)(2,1)S(1)}) fusion(f32[320]{0:T(512)S(1)} %reduce.34, bf16[1,9,320,8,128]{4,2,1,3,0:T(8,128)(2,1)} %copy-done.3, bf16[320,9,320]{2,0,1:T(8,128)(2,1)} %all-gather.7.cloned.1.call-done), kind=kOutput, calls=%fused_computation.26 | convolution fusion | flops 1889402368 | bytes 8400640 | tf_op jit(solution)/shard_map/otc,ntchw->nohw/dot_general | solution.py:84
  58.0 9.6 %all-reduce.6 = (f32[1,32]{1,0:T(1,128)S(1)}, f32[1,32]{1,0:T(1,128)S(1)}) all-reduce(f32[1,32]{1,0:T(1,128)S(1)} %bitcast.377, f32[1,32]{1,0:T(1,128)S(1)} %bitcast.373), channel_id=1, replica_groups=mesh['groups'=2,'rows'=4,'zero'=4] {'rows'}, use_global_device_ids=true, to_apply=%region_11.12 | all-reduce | flops 64 | bytes 512 | tf_op jit(solution)/shard_map/psum | solution.py:47
  68.0 7.3 %fusion.83 = (f32[320]{0:T(512)S(1)}, f32[320]{0:T(512)S(1)}, f32[320]{0:T(512)S(1)}, f32[320]{0:T(512)S(1)}, f32[1,320,8,128]{3,1,2,0:T(8,128)}) fusion(bf16[1,8,128,320]{2,3,1,0:T(8,128)(2,1)S(1)} %get-tuple-element.64, f32[320]{0:T(512)S(1)} %mul.235, f32[320]{0:T(512)S(1)} %sub.127, f32[320]{0:T(512)S(1)} %get-tuple-element.68, ...), kind=kOutput, calls=%fused_computation.64 | convolution fusion | flops 1893989376 | bytes 9717760 | tf_op jit(solution)/shard_map/otc,ntohw->nchw/dot_general | solution.py:93
  75.7 9.4 %all-reduce.5 = (f32[1,32]{1,0:T(1,128)S(1)}, f32[1,32]{1,0:T(1,128)S(1)}) all-reduce(f32[1,32]{1,0:T(1,128)S(1)} %bitcast.378, f32[1,32]{1,0:T(1,128)S(1)} %bitcast.374), channel_id=1, replica_groups=mesh['groups'=2,'rows'=4,'zero'=4] {'rows'}, use_global_device_ids=true, to_apply=%region_17.18 | all-reduce | flops 64 | bytes 512 | tf_op jit(solution)/shard_map/psum | solution.py:63
  85.4 2.3 fusion.154
  87.7 8.1 %fusion.17 = f32[320,9,320]{2,0,1:T(8,128)} fusion(bf16[1,9,320,8,128]{4,2,1,3,0:T(8,128)(2,1)} %copy-done.3, bf16[1,320,8,128]{3,1,2,0:T(8,128)(2,1)S(1)} %get-tuple-element.50), kind=kOutput, calls=%fused_computation.23 | convolution fusion | flops 1887436800 | bytes 10240000 | tf_op jit(solution)/shard_map/nohw,ntchw->otc/dot_general | solution.py:103
  95.9 2.9 collective-permute-start.2
  98.8 1.3 collective-permute-start.3
  100.9 4.3 %collective-permute-done.3 = bf16[1,320,1,128]{3,1,2,0:T(8,128)(2,1)S(1)} collective-permute-done((bf16[1,320,1,128]{3,1,2,0:T(8,128)(2,1)S(1)}, bf16[1,320,1,128]{3,1,2,0:T(8,128)(2,1)S(1)}, u32[]{:S(2)}, u32[]{:S(2)}) %collective-permute-start.3) | collective-permute-done | bytes 81952 | tf_op jit(solution)/shard_map/ppermute | solution.py:20
  105.2 0.9 select_maximum_fusion.4
  107.9 4.9 %fusion.4 = f32[9,320,320,1]{2,1,3,0:T(8,128)} fusion(bf16[1,9,320,8,128]{4,2,3,1,0:T(8,128)(2,1)S(1)} %fusion.131, bf16[320,8,128]{2,1,0:T(8,128)(2,1)S(1)} %bitcast.367), kind=kOutput, calls=%fused_computation.4 | convolution fusion | flops 1887436800 | bytes 10240000 | tf_op jit(solution)/shard_map/nohw,ntchw->otc/dot_general | solution.py:103
  112.7 6.1 %copy.102 = f32[320,2880]{1,0:T(8,128)} copy(f32[320,2880]{0,1:T(8,128)} %bitcast.370) | data formatting | bytes 7372800
  118.9 21.8 %reduce-scatter.5.cloned.1.call-done = f32[80,9,320]{2,0,1:T(8,128)} async-done(((f32[320,9,320]{2,0,1:T(8,128)}), f32[80,9,320]{2,0,1:T(8,128)}) %reduce-scatter.5.cloned.1.call-update) | async-done | bytes 921616 | tf_op jit(solution)/shard_map/reduce_scatter | solution.py:102
  140.7 44.4 %reduce-scatter.7.cloned.1.call-done = f32[80,2880]{1,0:T(8,128)} async-done(((f32[320,2880]{1,0:T(8,128)}), f32[80,2880]{1,0:T(8,128)}) %reduce-scatter.7.cloned.1.call-update) | async-done | bytes 921616
  185.1 1.6 copy.103
  186.8 1.5 copy.91
  188.3 3.4 collective-permute-start.6
  191.7 1.5 collective-permute-start.7
  193.8 5.3 %collective-permute-done.7 = bf16[1,320,1,128]{3,1,2,0:T(8,128)(2,1)S(1)} collective-permute-done((bf16[1,320,1,128]{3,1,2,0:T(8,128)(2,1)S(1)}, bf16[1,320,1,128]{3,1,2,0:T(8,128)(2,1)S(1)}, u32[]{:S(2)}, u32[]{:S(2)}) %collective-permute-start.7) | collective-permute-done | bytes 81952 | tf_op jit(solution)/shard_map/ppermute | solution.py:20
  201.7 1.4 copy-done.6
  203.1 3.0 fusion.105
  206.5 10.6 %all-reduce.4 = (f32[1,32]{1,0:T(1,128)S(1)}, f32[1,32]{1,0:T(1,128)S(1)}, f32[1,320]{1,0:T(1,128)}) all-reduce(f32[1,32]{1,0:T(1,128)S(1)} %bitcast.372, f32[1,32]{1,0:T(1,128)S(1)} %bitcast.371, f32[1,320]{1,0:T(1,128)S(1)} %reduce_sum.242), channel_id=1, replica_groups=mesh['groups'=2,'rows'=4,'zero'=4] {'rows'}, use_global_device_ids=true, to_apply=%region_23.24 | all-reduce | flops 384 | bytes 3072 | tf_op jit(solution)/shard_map/psum | solution.py:63
  218.1 1.3 copy.93
  219.4 4.9 %fusion.59 = bf16[1,320,8,128]{3,1,2,0:T(8,128)(2,1)S(1)} fusion(bf16[1,9,320,8,128]{4,2,3,1,0:T(8,128)(2,1)} %copy-done.4, bf16[320,9,320]{2,0,1:T(8,128)(2,1)S(1)} %copy-done.7, bf16[1,320,8,128]{3,2,1,0:T(8,128)(2,1)S(1)} %copy-done), kind=kOutput, calls=%fused_computation.44 | convolution fusion | flops 1888419840 | bytes 9052160 | tf_op jit(solution)/shard_map/otc,ntchw->nohw/dot_general | solution.py:84
  224.4 1.3 copy.92
  225.6 32.3 %psum.79 = f32[4,320]{1,0:T(4,128)} all-reduce(f32[4,320]{1,0:T(4,128)S(1)} %pad_maximum_fusion.8), channel_id=1, replica_groups=mesh['groups'=2,'rows'=4,'zero'=4] {'rows','zero'}, use_global_device_ids=true, to_apply=%region_34.35 | all-reduce | flops 1280 | bytes 10240 | tf_op jit(solution)/shard_map/psum | solution.py:149
  257.9 14.0 %all-gather.11.cloned.1.call-done = f32[320,9,320]{2,0,1:T(8,128)} async-done(((f32[80,9,320]{2,0,1:T(8,128)}), f32[320,9,320]{2,0,1:T(8,128)}) %all-gather.11.cloned.1.call-update) | async-done | bytes 3686416 | tf_op jit(solution)/shard_map/all_gather | solution.py:9
  271.9 3.6 reduce_sum.243
  275.5 81.6 %all-gather.13.cloned.1.call-done = f32[320,9,320]{2,0,1:T(8,128)} async-done(((f32[80,9,320]{2,0,1:T(8,128)}), f32[320,9,320]{2,0,1:T(8,128)}) %all-gather.13.cloned.1.call-update) | async-done | bytes 3686416 | tf_op jit(solution)/shard_map/all_gather | solution.py:9
  357.1 3.6 reduce_sum.244
  (115 shorter events, 15.3 us)
Async XLA Ops:
  7.2 17.3 %copy-start = (bf16[1,320,8,128]{3,2,1,0:T(8,128)(2,1)S(1)}, bf16[1,320,8,128]{3,2,1,0:T(8,128)(2,1)}, u32[]{:S(2)}) copy-start(bf16[1,320,8,128]{3,2,1,0:T(8,128)(2,1)} %param.7) | copy-start | bytes 1966084
  7.2 20.5 %copy-start.1 = (bf16[1,320,8,128]{3,2,1,0:T(8,128)(2,1)S(1)}, bf16[1,320,8,128]{3,2,1,0:T(8,128)(2,1)}, u32[]{:S(2)}) copy-start(bf16[1,320,8,128]{3,2,1,0:T(8,128)(2,1)} %param.13) | copy-start | bytes 1966084
  7.2 44.6 %all-gather.7.cloned.1.call-start = ((), (), s32[]{:S(2)}) async-start(), calls=%async_computation.2 | async-start | bytes 2764800 | tf_op jit(solution)/shard_map/all_gather | solution.py:86
  7.9 60.1 %all-gather.9.cloned.1.call-start = ((), (), s32[]{:S(2)}) async-start(), calls=%async_computation.3 | async-start | bytes 2764800 | tf_op jit(solution)/shard_map/all_gather | solution.py:86
  24.4 9.3 %copy-start.5 = (f32[1,320]{1,0:T(1,128)S(1)}, f32[1,320]{1,0:T(1,128)}, u32[]{:S(2)}) copy-start(f32[1,320]{1,0:T(1,128)} %param.8) | copy-start | bytes 3844
  25.1 8.7 %collective-permute-start = (bf16[1,320,1,128]{3,1,2,0:T(8,128)(2,1)S(1)}, bf16[1,320,1,128]{3,1,2,0:T(8,128)(2,1)S(1)}, u32[]{:S(2)}, u32[]{:S(2)}) collective-permute-start(bf16[1,320,1,128]{3,1,2,0:T(8,128)(2,1)S(1)} %get-tuple-element.58), channel_id=1, source_target_pairs={{0,4},{4,8},{8,12},{1,5},{5,9},{9,13},{2,6},{6,10},{10,14},{3,7},{... | collective-permute-start | bytes 245768 | tf_op jit(solution)/shard_map/ppermute | solution.py:19
  26.4 7.4 %collective-permute-start.1 = (bf16[1,320,1,128]{3,1,2,0:T(8,128)(2,1)S(1)}, bf16[1,320,1,128]{3,1,2,0:T(8,128)(2,1)S(1)}, u32[]{:S(2)}, u32[]{:S(2)}) collective-permute-start(bf16[1,320,1,128]{3,1,2,0:T(8,128)(2,1)S(1)} %get-tuple-element.59), channel_id=1, source_target_pairs={{4,0},{8,4},{12,8},{5,1},{9,5},{13,9},{6,2},{10,6},{14,10},{7,3},{... | collective-permute-start | bytes 245768 | tf_op jit(solution)/shard_map/ppermute | solution.py:20
  27.8 8.9 %collective-permute-start.4 = (bf16[1,320,1,128]{3,1,2,0:T(8,128)(2,1)S(1)}, bf16[1,320,1,128]{3,1,2,0:T(8,128)(2,1)S(1)}, u32[]{:S(2)}, u32[]{:S(2)}) collective-permute-start(bf16[1,320,1,128]{3,1,2,0:T(8,128)(2,1)S(1)} %get-tuple-element.54), channel_id=1, source_target_pairs={{0,4},{4,8},{8,12},{1,5},{5,9},{9,13},{2,6},{6,10},{10,14},{3,7},{... | collective-permute-start | bytes 245768 | tf_op jit(solution)/shard_map/ppermute | solution.py:19
  32.4 6.3 %collective-permute-start.5 = (bf16[1,320,1,128]{3,1,2,0:T(8,128)(2,1)S(1)}, bf16[1,320,1,128]{3,1,2,0:T(8,128)(2,1)S(1)}, u32[]{:S(2)}, u32[]{:S(2)}) collective-permute-start(bf16[1,320,1,128]{3,1,2,0:T(8,128)(2,1)S(1)} %get-tuple-element.55), channel_id=1, source_target_pairs={{4,0},{8,4},{12,8},{5,1},{9,5},{13,9},{6,2},{10,6},{14,10},{7,3},{... | collective-permute-start | bytes 245768 | tf_op jit(solution)/shard_map/ppermute | solution.py:20
  33.7 106.9 %reduce-scatter.5.cloned.1.call-start = ((), (), s32[]{:S(2)}) async-start(), calls=%async_computation.4 | async-start | bytes 5529600 | tf_op jit(solution)/shard_map/reduce_scatter | solution.py:102
  48.3 2.5 copy-start.3
  95.8 89.3 %reduce-scatter.7.cloned.1.call-start = ((), (), s32[]{:S(2)}) async-start(), calls=%async_computation.7 | async-start | bytes 4710400
  95.9 4.9 %collective-permute-start.2 = (bf16[1,320,1,128]{3,1,2,0:T(8,128)(2,1)S(1)}, bf16[1,320,1,128]{3,1,2,0:T(8,128)(2,1)S(1)}, u32[]{:S(2)}, u32[]{:S(2)}) collective-permute-start(bf16[1,320,1,128]{3,1,2,0:T(8,128)(2,1)S(1)} %get-tuple-element.56), channel_id=1, source_target_pairs={{0,4},{4,8},{8,12},{1,5},{5,9},{9,13},{2,6},{6,10},{10,14},{3,7},{... | collective-permute-start | bytes 245768 | tf_op jit(solution)/shard_map/ppermute | solution.py:19
  98.8 6.3 %collective-permute-start.3 = (bf16[1,320,1,128]{3,1,2,0:T(8,128)(2,1)S(1)}, bf16[1,320,1,128]{3,1,2,0:T(8,128)(2,1)S(1)}, u32[]{:S(2)}, u32[]{:S(2)}) collective-permute-start(bf16[1,320,1,128]{3,1,2,0:T(8,128)(2,1)S(1)} %get-tuple-element.57), channel_id=1, source_target_pairs={{4,0},{8,4},{12,8},{5,1},{9,5},{13,9},{6,2},{10,6},{14,10},{7,3},{... | collective-permute-start | bytes 245768 | tf_op jit(solution)/shard_map/ppermute | solution.py:20
  107.9 4.9 %copy-start.4 = (bf16[1,9,320,8,128]{4,2,3,1,0:T(8,128)(2,1)}, bf16[1,9,320,8,128]{4,2,3,1,0:T(8,128)(2,1)S(1)}, u32[]{:S(2)}) copy-start(bf16[1,9,320,8,128]{4,2,3,1,0:T(8,128)(2,1)S(1)} %fusion.131) | copy-start | bytes 17694724
  118.8 153.0 %all-gather.11.cloned.1.call-start = ((), (), s32[]{:S(2)}) async-start(), calls=%async_computation.5 | async-start | bytes 5529600 | tf_op jit(solution)/shard_map/all_gather | solution.py:9
  140.7 216.4 %all-gather.13.cloned.1.call-start = ((), (), s32[]{:S(2)}) async-start(), calls=%async_computation.6 | async-start | bytes 5529600 | tf_op jit(solution)/shard_map/all_gather | solution.py:9
  188.3 5.4 %collective-permute-start.6 = (bf16[1,320,1,128]{3,1,2,0:T(8,128)(2,1)S(1)}, bf16[1,320,1,128]{3,1,2,0:T(8,128)(2,1)S(1)}, u32[]{:S(2)}, u32[]{:S(2)}) collective-permute-start(bf16[1,320,1,128]{3,1,2,0:T(8,128)(2,1)S(1)} %get-tuple-element.52), channel_id=1, source_target_pairs={{0,4},{4,8},{8,12},{1,5},{5,9},{9,13},{2,6},{6,10},{10,14},{3,7},{... | collective-permute-start | bytes 245768 | tf_op jit(solution)/shard_map/ppermute | solution.py:19
  191.7 7.3 %collective-permute-start.7 = (bf16[1,320,1,128]{3,1,2,0:T(8,128)(2,1)S(1)}, bf16[1,320,1,128]{3,1,2,0:T(8,128)(2,1)S(1)}, u32[]{:S(2)}, u32[]{:S(2)}) collective-permute-start(bf16[1,320,1,128]{3,1,2,0:T(8,128)(2,1)S(1)} %get-tuple-element.53), channel_id=1, source_target_pairs={{4,0},{8,4},{12,8},{5,1},{9,5},{13,9},{6,2},{10,6},{14,10},{7,3},{... | collective-permute-start | bytes 245768 | tf_op jit(solution)/shard_map/ppermute | solution.py:20
  201.4 1.6 copy-start.6
  203.0 14.4 %copy-start.2 = (bf16[1,320,8,128]{3,2,1,0:T(8,128)(2,1)S(1)}, bf16[1,320,8,128]{3,2,1,0:T(8,128)(2,1)}, u32[]{:S(2)}) copy-start(bf16[1,320,8,128]{3,2,1,0:T(8,128)(2,1)} %param.13) | copy-start | bytes 1966084
  217.5 1.9 copy-start.7
Sparse Core Ops, SparseCore 0:
  9.6 25.9 all-gather.6
  37.1 23.2 all-gather.8
  96.0 44.6 reduce-scatter.4
  143.2 41.8 reduce-scatter.6
  186.5 85.3 all-gather.10
  273.9 83.1 all-gather.12
